TPU v7x, 128 devices: a whole 4x4x4 slice. The times are simulated.
128 devices in a mesh: lat: 8 (over x_lo, y), lon: 16 (over z, x_hi, core).
Axes of the slice: x: 4 (x_hi: 2, x_lo: 2; x = x_hi * 2 + x_lo), y: 4, z: 4, core: 2. Of those that a mesh axis runs over, the one named last changes fastest.
Arguments:
- grad_rows: bfloat16 [131072, 128], P(('lat', 'lon')), may hold values from -6 to 6
- owner: int32 [131072, 1], P(('lat', 'lon')), may hold values from 0 to 127; in each aligned block of 1024 rows (0 to 1023, 1024 to 2047, ...) at most 16 rows name the same one
- lat_offset: int32 [131072], P(('lat', 'lon')), may hold values from 0 to 63
- lon_offset: int32 [131072], P(('lat', 'lon')), may hold values from 0 to 127
- position: bfloat16 [131072, 2], P(('lat', 'lon')), may hold values from 0 to 1
- live_count: int32 [128], P(('lat', 'lon')), may hold values from 512 to 1024
- features: bfloat16 [512, 2048, 128], P('lat', 'lon'), may hold values from -6 to 6
- conv_weight: bfloat16 [3, 3, 128, 128], replicated, may hold values from -0.1875 to 0.1875
Outputs:
- input_grad: bfloat16 [512, 2048, 128], P('lat', 'lon')
- weight_grad: float32 [3, 3, 128, 128], replicated
Inputs may be any that keep to these rules, and one draw needn't show every extreme that they name: `owner`: among the 1024 rows of one device no tile is named more than 16 times, a bound that some block reaches. `live_count`: entry k counts the real rows among the rows of device k, which come first.
All inputs are finite; a program needn't handle non-finite values.
Results may differ from a plain program's by a relative error of at most 0.012.
Values may be sent and summed in bfloat16 or wider, within the bound.
No kernel may reach another device: no remote copies, remote signals or barrier semaphores. Data moves between devices by JAX's collectives and lax.ppermute only.
A program may use at most 128 MiB of HBM per device.

v0:
```python
import math
import jax
import jax.numpy as jnp
from jax import lax
from jax.sharding import PartitionSpec as P

rbf_scale = 1.5


def padded_2(cells, sides, width, closed):
    for axis, dim in sides:
        count = lax.axis_size(axis)
        ends = count if closed else count - 1
        head = lax.slice_in_dim(cells, 0, width, axis=dim)
        tail = lax.slice_in_dim(cells, cells.shape[dim] - width, cells.shape[dim], axis=dim)
        cells = jnp.concatenate(
            [
                lax.ppermute(tail, axis, [(i, (i + 1) % count) for i in range(ends)]),
                cells,
                lax.ppermute(head, axis, [((i + 1) % count, i) for i in range(ends)]),
            ],
            axis=dim,
        )
    return cells


def cut_along(value, dim, count):
    before, after = (value.shape[:dim], value.shape[dim + 1 :])
    return jnp.moveaxis(value.reshape(*before, count, -1, *after), dim, 0)


def in_order(parts, dim):
    shape = list(parts.shape[1:])
    shape[dim] *= parts.shape[0]
    return jnp.moveaxis(parts, 0, dim).reshape(shape)


def one_exchange(value, axis, axes, splits, concats):
    sizes = [lax.axis_size(a) for a in axes]
    parts = cut_along(value, splits[0], sizes[0])
    parts = jnp.moveaxis(cut_along(parts, splits[1] + 1, sizes[1]), 0, 1)
    inside = parts.shape[2:]
    parts = parts.reshape(-1, *inside)
    parts = lax.all_to_all(parts, axis, split_axis=0, concat_axis=0, tiled=True)
    parts = in_order(parts.reshape(*sizes, *inside), concats[0] + 1)
    return in_order(parts, concats[1])


def profile(frac):
    tap_index = jnp.arange(8).astype(frac.dtype)
    return jnp.exp(
        -jnp.square(tap_index[None, :] - 3.0 - frac[:, None]) / (2.0 * rbf_scale * rbf_scale)
    )


def clear_rim(padded):
    lat_index = lax.axis_index("lat")
    lat_count = lax.axis_size("lat")
    row_line = jnp.arange(padded.shape[0], dtype=jnp.int32)
    masked = (row_line == 0) & (lat_index == 0) | (row_line == padded.shape[0] - 1) & (
        lat_index == lat_count - 1
    )
    return jnp.where(masked[:, None, None], jnp.zeros_like(padded), padded)


def tap_matrix(offsets, weights, extent):
    tap_ints = jnp.arange(8, dtype=jnp.int32)
    cells = offsets[:, None] + tap_ints[None, :] + 1
    line = jnp.arange(extent, dtype=jnp.int32)
    picked = jnp.where(
        cells[:, :, None] == line[None, None, :], weights.astype(jnp.float32)[:, :, None], 0.0
    )
    return jnp.sum(picked, axis=1).astype(jnp.bfloat16)


def shards(grad_rows, owner, lat_offset, lon_offset, position, live_count, features, conv_weight):
    lat_total = lax.axis_size("lat")
    lon_total = lax.axis_size("lon")
    device_total = lat_total * lon_total
    row_total = grad_rows.shape[0]
    channels = grad_rows.shape[1]
    tile_lat = features.shape[0]
    tile_lon = features.shape[1]
    capacity = max(2, 2 * row_total // device_total)
    input_padded = clear_rim(padded_2(features, (("lat", 0), ("lon", 1)), 1, True))
    owner_tile = owner[:, 0]
    is_live = jnp.arange(row_total, dtype=jnp.int32) < live_count[0]
    matches = (
        (owner_tile[:, None] == jnp.arange(device_total, dtype=jnp.int32)[None, :])
        & is_live[:, None]
    ).astype(jnp.int32)
    earlier = jnp.cumsum(matches, axis=0) - matches
    slot_rank = jnp.sum(earlier * matches, axis=1)
    slot_index = jnp.where(is_live, owner_tile * capacity + slot_rank, device_total * capacity)
    outgoing = (
        jnp.zeros((device_total * capacity, channels), jnp.bfloat16)
        .at[slot_index]
        .set(grad_rows, mode="drop")
    )
    geometry = jnp.stack(
        [
            position[:, 0],
            position[:, 1],
            lat_offset.astype(jnp.bfloat16),
            lon_offset.astype(jnp.bfloat16),
        ],
        axis=1,
    )
    place_out = (
        jnp.zeros((device_total * capacity, 4), jnp.bfloat16)
        .at[slot_index]
        .set(geometry, mode="drop")
    )
    incoming, place_in = (
        one_exchange(
            outgoing.reshape(lat_total, lon_total, capacity, channels),
            ("lat", "lon"),
            ("lat", "lon"),
            (0, 1),
            (0, 1),
        ),
        one_exchange(
            place_out.reshape(lat_total, lon_total, capacity, 4),
            ("lat", "lon"),
            ("lat", "lon"),
            (0, 1),
            (0, 1),
        ),
    )
    incoming = incoming.reshape(-1, channels)
    place_in = place_in.reshape(-1, 4).astype(jnp.float32)
    padded_lat = tile_lat + 8
    padded_lon = tile_lon + 8
    slot_total = incoming.shape[0]
    block_rows = math.gcd(slot_total, 256)

    def accumulate(canvas, payload):
        rows_blk, place_blk = payload
        lat_weight = profile(place_blk[:, 0]).astype(jnp.bfloat16)
        lon_weight = profile(place_blk[:, 1]).astype(jnp.bfloat16)
        lat_matrix = tap_matrix(place_blk[:, 2].astype(jnp.int32), lat_weight, padded_lat)
        lon_matrix = tap_matrix(place_blk[:, 3].astype(jnp.int32), lon_weight, padded_lon)
        spread = (lon_matrix[:, :, None] * rows_blk[:, None, :]).reshape(
            rows_blk.shape[0], padded_lon * channels
        )
        canvas = canvas + lax.dot_general(
            lat_matrix, spread, (((0,), (0,)), ((), ())), preferred_element_type=jnp.float32
        )
        return (canvas, None)

    canvas, _ = lax.scan(
        accumulate,
        jnp.zeros((padded_lat, padded_lon * channels), jnp.float32),
        (incoming.reshape(-1, block_rows, channels), place_in.reshape(-1, block_rows, 4)),
    )
    canvas = canvas.reshape(padded_lat, padded_lon, channels)
    edge_rows = jnp.concatenate([canvas[:5], canvas[-5:]], axis=0)
    edge_rows = padded_2(edge_rows.astype(jnp.bfloat16), (("lat", 0),), 5, False).astype(
        edge_rows.dtype
    )
    inner = canvas[4:-4]
    inner = inner.at[:4].add(edge_rows[1:5]).at[-4:].add(edge_rows[15:19])
    rim_top = edge_rows[0] + canvas[3]
    rim_bottom = canvas[-4] + edge_rows[19]
    tall = jnp.concatenate([rim_top[None], inner, rim_bottom[None]], axis=0)
    side_cols = jnp.concatenate([tall[:, :5], tall[:, -5:]], axis=1)
    side_cols = padded_2(side_cols.astype(jnp.bfloat16), (("lon", 1),), 5, True).astype(
        side_cols.dtype
    )
    middle = tall[:, 4:-4]
    middle = middle.at[:, :4].add(side_cols[:, 1:5]).at[:, -4:].add(side_cols[:, 15:19])
    rim_left = side_cols[:, 0] + tall[:, 3]
    rim_right = tall[:, -4] + side_cols[:, 19]
    whole = jnp.concatenate([rim_left[:, None], middle, rim_right[:, None]], axis=1)
    grid_padded = clear_rim(whole.astype(jnp.bfloat16))
    grid_grad = grid_padded[1:-1, 1:-1]
    flat_grad = grid_grad.reshape(-1, channels)
    input_grad = jnp.zeros((tile_lat * tile_lon, channels), jnp.float32)
    weight_parts = []
    for a in range(3):
        for b in range(3):
            shifted = grid_padded[2 - a : 2 - a + tile_lat, 2 - b : 2 - b + tile_lon].reshape(
                -1, channels
            )
            input_grad = input_grad + lax.dot_general(
                shifted,
                conv_weight[a, b],
                (((1,), (1,)), ((), ())),
                preferred_element_type=jnp.float32,
            )
            window = input_padded[a : a + tile_lat, b : b + tile_lon].reshape(-1, channels)
            weight_parts.append(
                lax.dot_general(
                    window, flat_grad, (((0,), (0,)), ((), ())), preferred_element_type=jnp.float32
                )
            )
    weight_grad = lax.psum(
        jnp.stack(weight_parts).reshape(3, 3, channels, channels), ("lat", "lon")
    )
    return (input_grad.reshape(tile_lat, tile_lon, channels).astype(jnp.bfloat16), weight_grad)


def solution(mesh):
    placed = (
        P(("lat", "lon"), None),
        P(("lat", "lon"), None),
        P(("lat", "lon")),
        P(("lat", "lon")),
        P(("lat", "lon"), None),
        P(("lat", "lon")),
        P("lat", "lon", None),
        P(),
    )
    return jax.shard_map(
        shards, mesh=mesh, in_specs=placed, out_specs=(P("lat", "lon", None), P()), check_vma=False
    )
```

profile of v0, /device:TPU:1, one launch (start us, length us, event | category | flops | bytes accessed | tf_op | source)
XLA Modules:
  0.0 357.4 jit_solution(9674923736870181824)
XLA Ops:
  8.0 4.5 %collective-permute-start.5 = (bf16[1,128,128]{2,1,0:T(8,128)(2,1)S(1)}, bf16[1,128,128]{2,1,0:T(8,128)(2,1)S(1)}, u32[]{:S(2)}, u32[]{:S(2)}) collective-permute-start(bf16[1,128,128]{2,1,0:T(8,128)(2,1)S(1)} %get-tuple-element.168), channel_id=1, source_target_pairs={{16,0},{32,16},{48,32},{64,48},{80,64},{96,80},{112,96},{0,112},{1... | collective-permute-start | bytes 98312 | tf_op jit(solution)/shard_map/ppermute | solution.py:20
  22.2 11.0 %all-to-all-start = ((bf16[128,1,1,16,4]{3,4,2,1,0:T(4,128)(2,1)}), bf16[128,1,1,16,4]{3,4,2,1,0:T(4,128)(2,1)S(1)}, u32[]{:S(2)}, u32[]{:S(2)}) async-start(bf16[128,1,1,16,4]{3,4,2,1,0:T(4,128)(2,1)} %copy.87), calls=%async_computation | async-start | bytes 262144 | tf_op jit(solution)/shard_map/all_to_all | solution.py:44
  33.2 4.3 %scatter_custom_fusion.1 = bf16[2048,128]{1,0:T(8,128)(2,1)} fusion(s32[1024]{0:T(1024)S(1)} %bitcast.226, bf16[1024,128]{1,0:T(8,128)(2,1)} %param.18, bf16[]{:T(256)} %constant.168.clone.1), kind=kCustom, calls=%fused_computation.87 | custom fusion | bytes 524800 | tf_op jit(solution)/shard_map/scatter | solution.py:98
  37.5 5.6 %all-to-all-done = bf16[128,1,1,16,4]{3,4,2,1,0:T(4,128)(2,1)S(1)} async-done(((bf16[128,1,1,16,4]{3,4,2,1,0:T(4,128)(2,1)}), bf16[128,1,1,16,4]{3,4,2,1,0:T(4,128)(2,1)S(1)}, u32[]{:S(2)}, u32[]{:S(2)}) %all-to-all-start) | async-done | bytes 16416 | tf_op jit(solution)/shard_map/all_to_all | solution.py:44
  43.1 4.2 %all-to-all-start.1 = ((bf16[128,1,1,16,128]{4,3,2,1,0:T(8,128)(2,1)}), bf16[128,1,1,16,128]{4,3,2,1,0:T(8,128)(2,1)S(1)}, u32[]{:S(2)}, u32[]{:S(2)}) async-start(bf16[128,1,1,16,128]{4,3,2,1,0:T(8,128)(2,1)} %bitcast.13), calls=%async_computation.1 | async-start | bytes 1048576 | tf_op jit(solution)/shard_map/all_to_all | solution.py:44
  53.2 8.2 %all-to-all-done.1 = bf16[128,1,1,16,128]{4,3,2,1,0:T(8,128)(2,1)S(1)} async-done(((bf16[128,1,1,16,128]{4,3,2,1,0:T(8,128)(2,1)}), bf16[128,1,1,16,128]{4,3,2,1,0:T(8,128)(2,1)S(1)}, u32[]{:S(2)}, u32[]{:S(2)}) %all-to-all-start.1) | async-done | bytes 524320 | tf_op jit(solution)/shard_map/all_to_all | solution.py:44
  61.4 91.8 %while.17 = (s32[]{:T(128)}, f32[72,17408]{1,0:T(8,128)}, f32[8,256,4]{1,2,0:T(4,128)S(1)}, bf16[8,256,128]{2,1,0:T(8,128)(2,1)S(1)}, s32[]{:T(128)}, /*index=5*/s32[]{:T(128)}) while((s32[]{:T(128)}, f32[72,17408]{1,0:T(8,128)}, f32[8,256,4]{1,2,0:T(4,128)S(1)}, bf16[8,256,128]{2,1,0:T(8,128)(2,1)S(1)}, s32[]{:T(128)}, ...), condition=%wide.region_8.9_spmd.clone, body=%wide.region_5.8_spmd.clone.sunk | while | flops 649949696 | bytes 63582440 | solution.py:151
  61.9 5.2 %broadcast_multiply_fusion.2 = bf16[256,136,128]{2,1,0:T(8,128)(2,1)S(1)} fusion(bf16[256,128]{1,0:T(8,128)(2,1)S(1)} %dynamic-slice_bitcast_fusion.4, bf16[256,136]{1,0:T(8,128)(2,1)S(1)} %copy.129), kind=kLoop, calls=%fused_computation.5.clone.1 | loop fusion | flops 4456448 | bytes 9048064 | tf_op jit(solution)/shard_map/while/body/eval_jaxpr/mul | solution.py:143
  73.4 5.2 %broadcast_multiply_fusion.2 = bf16[256,136,128]{2,1,0:T(8,128)(2,1)S(1)} fusion(bf16[256,128]{1,0:T(8,128)(2,1)S(1)} %dynamic-slice_bitcast_fusion.4, bf16[256,136]{1,0:T(8,128)(2,1)S(1)} %copy.129), kind=kLoop, calls=%fused_computation.5.clone.1 | loop fusion | flops 4456448 | bytes 9048064 | tf_op jit(solution)/shard_map/while/body/eval_jaxpr/mul | solution.py:143
  84.8 5.2 %broadcast_multiply_fusion.2 = bf16[256,136,128]{2,1,0:T(8,128)(2,1)S(1)} fusion(bf16[256,128]{1,0:T(8,128)(2,1)S(1)} %dynamic-slice_bitcast_fusion.4, bf16[256,136]{1,0:T(8,128)(2,1)S(1)} %copy.129), kind=kLoop, calls=%fused_computation.5.clone.1 | loop fusion | flops 4456448 | bytes 9048064 | tf_op jit(solution)/shard_map/while/body/eval_jaxpr/mul | solution.py:143
  90.1 3.6 convolution_add_fusion.10
  96.3 5.2 %broadcast_multiply_fusion.2 = bf16[256,136,128]{2,1,0:T(8,128)(2,1)S(1)} fusion(bf16[256,128]{1,0:T(8,128)(2,1)S(1)} %dynamic-slice_bitcast_fusion.4, bf16[256,136]{1,0:T(8,128)(2,1)S(1)} %copy.129), kind=kLoop, calls=%fused_computation.5.clone.1 | loop fusion | flops 4456448 | bytes 9048064 | tf_op jit(solution)/shard_map/while/body/eval_jaxpr/mul | solution.py:143
  101.5 3.6 convolution_add_fusion.10
  107.8 5.2 %broadcast_multiply_fusion.2 = bf16[256,136,128]{2,1,0:T(8,128)(2,1)S(1)} fusion(bf16[256,128]{1,0:T(8,128)(2,1)S(1)} %dynamic-slice_bitcast_fusion.4, bf16[256,136]{1,0:T(8,128)(2,1)S(1)} %copy.129), kind=kLoop, calls=%fused_computation.5.clone.1 | loop fusion | flops 4456448 | bytes 9048064 | tf_op jit(solution)/shard_map/while/body/eval_jaxpr/mul | solution.py:143
  113.0 3.6 convolution_add_fusion.10
  119.3 5.2 %broadcast_multiply_fusion.2 = bf16[256,136,128]{2,1,0:T(8,128)(2,1)S(1)} fusion(bf16[256,128]{1,0:T(8,128)(2,1)S(1)} %dynamic-slice_bitcast_fusion.4, bf16[256,136]{1,0:T(8,128)(2,1)S(1)} %copy.129), kind=kLoop, calls=%fused_computation.5.clone.1 | loop fusion | flops 4456448 | bytes 9048064 | tf_op jit(solution)/shard_map/while/body/eval_jaxpr/mul | solution.py:143
  124.5 3.6 convolution_add_fusion.10
  130.8 5.2 %broadcast_multiply_fusion.2 = bf16[256,136,128]{2,1,0:T(8,128)(2,1)S(1)} fusion(bf16[256,128]{1,0:T(8,128)(2,1)S(1)} %dynamic-slice_bitcast_fusion.4, bf16[256,136]{1,0:T(8,128)(2,1)S(1)} %copy.129), kind=kLoop, calls=%fused_computation.5.clone.1 | loop fusion | flops 4456448 | bytes 9048064 | tf_op jit(solution)/shard_map/while/body/eval_jaxpr/mul | solution.py:143
  136.0 3.6 convolution_add_fusion.10
  142.2 5.2 %broadcast_multiply_fusion.2 = bf16[256,136,128]{2,1,0:T(8,128)(2,1)S(1)} fusion(bf16[256,128]{1,0:T(8,128)(2,1)S(1)} %dynamic-slice_bitcast_fusion.4, bf16[256,136]{1,0:T(8,128)(2,1)S(1)} %copy.129), kind=kLoop, calls=%fused_computation.5.clone.1 | loop fusion | flops 4456448 | bytes 9048064 | tf_op jit(solution)/shard_map/while/body/eval_jaxpr/mul | solution.py:143
  161.1 4.0 %collective-permute-start = (bf16[5,136,128]{2,1,0:T(8,128)(2,1)S(1)}, bf16[5,136,128]{2,1,0:T(8,128)(2,1)S(1)}, u32[]{:S(2)}, u32[]{:S(2)}) collective-permute-start(bf16[5,136,128]{2,1,0:T(8,128)(2,1)S(1)} %bitcast.203), channel_id=1, source_target_pairs={{0,16},{16,32},{32,48},{48,64},{64,80},{80,96},{96,112},{1,17},{17... | collective-permute-start | bytes 522248 | tf_op jit(solution)/shard_map/ppermute | solution.py:18
  172.8 4.2 %collective-permute-done.3 = bf16[66,5,128]{2,1,0:T(8,128)(2,1)S(1)} collective-permute-done((bf16[66,5,128]{2,1,0:T(8,128)(2,1)S(1)}, bf16[66,5,128]{2,1,0:T(8,128)(2,1)S(1)}, u32[]{:S(2)}, u32[]{:S(2)}) %collective-permute-start.3) | collective-permute-done | bytes 84512 | tf_op jit(solution)/shard_map/ppermute | solution.py:20
  181.1 7.0 %fusion.129 = (bf16[64,128,128]{2,1,0:T(8,128)(2,1)}, bf16[64,128,128]{2,1,0:T(8,128)(2,1)S(1)}, bf16[64,128,128]{2,1,0:T(8,128)(2,1)}, bf16[64,128,128]{2,1,0:T...) fusion(bf16[66,130,128]{2,1,0:T(8,128)(2,1)S(1)} %get-tuple-ele, ...), kind=kLoop, calls=%fused_computation.153 | loop fusion | bytes 37748736 | tf_op jit(solution)/shard_map/slice | solution.py:182
  214.3 134.3 %all-reduce.2.cloned.1.call-done = f32[3,3,128,128]{3,2,1,0:T(8,128)} async-done(((f32[3,3,128,128]{3,2,1,0:T(8,128)}), f32[3,3,128,128]{3,2,1,0:T(8,128)}) %all-reduce.2.cloned.1.call-update) | async-done | bytes 589840 | tf_op jit(solution)/shard_map/psum | solution.py:197
  (245 shorter events, 94.9 us)
Async XLA Ops:
  7.2 9.6 %copy-start.11 = (s32[1024,1]{0,1:T(1,128)S(1)}, s32[1024,1]{0,1:T(1,128)}, u32[]{:S(2)}) copy-start(s32[1024,1]{0,1:T(1,128)} %param.19) | copy-start | bytes 12292
  8.0 41.9 %collective-permute-start.5 = (bf16[1,128,128]{2,1,0:T(8,128)(2,1)S(1)}, bf16[1,128,128]{2,1,0:T(8,128)(2,1)S(1)}, u32[]{:S(2)}, u32[]{:S(2)}) collective-permute-start(bf16[1,128,128]{2,1,0:T(8,128)(2,1)S(1)} %get-tuple-element.168), channel_id=1, source_target_pairs={{16,0},{32,16},{48,32},{64,48},{80,64},{96,80},{112,96},{0,112},{1... | collective-permute-start | bytes 98312 | tf_op jit(solution)/shard_map/ppermute | solution.py:20
  12.5 35.4 %collective-permute-start.4 = (bf16[1,128,128]{2,1,0:T(8,128)(2,1)S(1)}, bf16[1,128,128]{2,1,0:T(8,128)(2,1)S(1)}, u32[]{:S(2)}, u32[]{:S(2)}) collective-permute-start(bf16[1,128,128]{2,1,0:T(8,128)(2,1)S(1)} %get-tuple-element.169), channel_id=1, source_target_pairs={{0,16},{16,32},{32,48},{48,64},{64,80},{80,96},{96,112},{112,0},{1... | collective-permute-start | bytes 98312 | tf_op jit(solution)/shard_map/ppermute | solution.py:18
  22.2 20.9 %all-to-all-start = ((bf16[128,1,1,16,4]{3,4,2,1,0:T(4,128)(2,1)}), bf16[128,1,1,16,4]{3,4,2,1,0:T(4,128)(2,1)S(1)}, u32[]{:S(2)}, u32[]{:S(2)}) async-start(bf16[128,1,1,16,4]{3,4,2,1,0:T(4,128)(2,1)} %copy.87), calls=%async_computation | async-start | bytes 262144 | tf_op jit(solution)/shard_map/all_to_all | solution.py:44
  43.1 18.3 %all-to-all-start.1 = ((bf16[128,1,1,16,128]{4,3,2,1,0:T(8,128)(2,1)}), bf16[128,1,1,16,128]{4,3,2,1,0:T(8,128)(2,1)S(1)}, u32[]{:S(2)}, u32[]{:S(2)}) async-start(bf16[128,1,1,16,128]{4,3,2,1,0:T(8,128)(2,1)} %bitcast.13), calls=%async_computation.1 | async-start | bytes 1048576 | tf_op jit(solution)/shard_map/all_to_all | solution.py:44
  47.3 301.3 %all-reduce.2.cloned.1.call-start = ((), (), s32[]{:S(2)}) async-start(), calls=%async_computation.2 | async-start | bytes 1179648 | tf_op jit(solution)/shard_map/psum | solution.py:197
  50.0 128.0 %collective-permute-start.6 = (bf16[66,1,128]{2,1,0:T(2,128)(2,1)S(1)}, bf16[66,1,128]{2,1,0:T(2,128)(2,1)S(1)}, u32[]{:S(2)}, u32[]{:S(2)}) collective-permute-start(bf16[66,1,128]{2,1,0:T(2,128)(2,1)S(1)} %get-tuple-element.166), channel_id=1, source_target_pairs={{0,1},{1,2},{2,3},{3,4},{4,5},{5,6},{6,7},{7,8},{8,9},{9,10},{10,1... | collective-permute-start | bytes 50696 | tf_op jit(solution)/shard_map/ppermute | solution.py:18
  53.2 124.8 %collective-permute-start.7 = (bf16[66,1,128]{2,1,0:T(2,128)(2,1)S(1)}, bf16[66,1,128]{2,1,0:T(2,128)(2,1)S(1)}, u32[]{:S(2)}, u32[]{:S(2)}) collective-permute-start(bf16[66,1,128]{2,1,0:T(2,128)(2,1)S(1)} %get-tuple-element.167), channel_id=1, source_target_pairs={{1,0},{2,1},{3,2},{4,3},{5,4},{6,5},{7,6},{8,7},{9,8},{10,9},{11,1... | collective-permute-start | bytes 50696 | tf_op jit(solution)/shard_map/ppermute | solution.py:20
  61.8 5.2 %slice-start = ((s8[5013504]{0:T(1024)(128)(4,1)}), s8[4194304]{0:T(1024)(128)(4,1)S(1)}, s32[]{:S(2)}) async-start(s8[5013504]{0:T(1024)(128)(4,1)} %bitcast.191), calls=%async_computation.3 | async-start | bytes 8388608 | tf_op jit(solution)/shard_map/while
  61.9 5.2 %slice-start.1 = ((s8[5013504]{0:T(1024)(128)(4,1)}), s8[819200]{0:T(1024)(128)(4,1)S(1)}, s32[]{:S(2)}) async-start(s8[5013504]{0:T(1024)(128)(4,1)} %bitcast.191), calls=%async_computation.4 | async-start | bytes 1638400 | tf_op jit(solution)/shard_map/while
  73.3 5.2 %slice-start = ((s8[5013504]{0:T(1024)(128)(4,1)}), s8[4194304]{0:T(1024)(128)(4,1)S(1)}, s32[]{:S(2)}) async-start(s8[5013504]{0:T(1024)(128)(4,1)} %bitcast.191), calls=%async_computation.3 | async-start | bytes 8388608 | tf_op jit(solution)/shard_map/while
  73.4 5.2 %slice-start.1 = ((s8[5013504]{0:T(1024)(128)(4,1)}), s8[819200]{0:T(1024)(128)(4,1)S(1)}, s32[]{:S(2)}) async-start(s8[5013504]{0:T(1024)(128)(4,1)} %bitcast.191), calls=%async_computation.4 | async-start | bytes 1638400 | tf_op jit(solution)/shard_map/while
  84.8 5.2 %slice-start = ((s8[5013504]{0:T(1024)(128)(4,1)}), s8[4194304]{0:T(1024)(128)(4,1)S(1)}, s32[]{:S(2)}) async-start(s8[5013504]{0:T(1024)(128)(4,1)} %bitcast.191), calls=%async_computation.3 | async-start | bytes 8388608 | tf_op jit(solution)/shard_map/while
  84.8 5.2 %slice-start.1 = ((s8[5013504]{0:T(1024)(128)(4,1)}), s8[819200]{0:T(1024)(128)(4,1)S(1)}, s32[]{:S(2)}) async-start(s8[5013504]{0:T(1024)(128)(4,1)} %bitcast.191), calls=%async_computation.4 | async-start | bytes 1638400 | tf_op jit(solution)/shard_map/while
  96.3 5.2 %slice-start = ((s8[5013504]{0:T(1024)(128)(4,1)}), s8[4194304]{0:T(1024)(128)(4,1)S(1)}, s32[]{:S(2)}) async-start(s8[5013504]{0:T(1024)(128)(4,1)} %bitcast.191), calls=%async_computation.3 | async-start | bytes 8388608 | tf_op jit(solution)/shard_map/while
  107.8 5.2 %slice-start = ((s8[5013504]{0:T(1024)(128)(4,1)}), s8[4194304]{0:T(1024)(128)(4,1)S(1)}, s32[]{:S(2)}) async-start(s8[5013504]{0:T(1024)(128)(4,1)} %bitcast.191), calls=%async_computation.3 | async-start | bytes 8388608 | tf_op jit(solution)/shard_map/while
  119.2 5.2 %slice-start = ((s8[5013504]{0:T(1024)(128)(4,1)}), s8[4194304]{0:T(1024)(128)(4,1)S(1)}, s32[]{:S(2)}) async-start(s8[5013504]{0:T(1024)(128)(4,1)} %bitcast.191), calls=%async_computation.3 | async-start | bytes 8388608 | tf_op jit(solution)/shard_map/while
  119.3 5.2 %slice-start.1 = ((s8[5013504]{0:T(1024)(128)(4,1)}), s8[819200]{0:T(1024)(128)(4,1)S(1)}, s32[]{:S(2)}) async-start(s8[5013504]{0:T(1024)(128)(4,1)} %bitcast.191), calls=%async_computation.4 | async-start | bytes 1638400 | tf_op jit(solution)/shard_map/while
  130.7 5.2 %slice-start = ((s8[5013504]{0:T(1024)(128)(4,1)}), s8[4194304]{0:T(1024)(128)(4,1)S(1)}, s32[]{:S(2)}) async-start(s8[5013504]{0:T(1024)(128)(4,1)} %bitcast.191), calls=%async_computation.3 | async-start | bytes 8388608 | tf_op jit(solution)/shard_map/while
  142.2 5.2 %slice-start = ((s8[5013504]{0:T(1024)(128)(4,1)}), s8[4194304]{0:T(1024)(128)(4,1)S(1)}, s32[]{:S(2)}) async-start(s8[5013504]{0:T(1024)(128)(4,1)} %bitcast.191), calls=%async_computation.3 | async-start | bytes 8388608 | tf_op jit(solution)/shard_map/while
  159.8 7.7 %collective-permute-start.1 = (bf16[5,136,128]{2,1,0:T(8,128)(2,1)S(1)}, bf16[5,136,128]{2,1,0:T(8,128)(2,1)S(1)}, u32[]{:S(2)}, u32[]{:S(2)}) collective-permute-start(bf16[5,136,128]{2,1,0:T(8,128)(2,1)S(1)} %bitcast.207), channel_id=1, source_target_pairs={{16,0},{32,16},{48,32},{64,48},{80,64},{96,80},{112,96},{17,1},{33... | collective-permute-start | bytes 522248 | tf_op jit(solution)/shard_map/ppermute | solution.py:20
  161.1 7.2 %collective-permute-start = (bf16[5,136,128]{2,1,0:T(8,128)(2,1)S(1)}, bf16[5,136,128]{2,1,0:T(8,128)(2,1)S(1)}, u32[]{:S(2)}, u32[]{:S(2)}) collective-permute-start(bf16[5,136,128]{2,1,0:T(8,128)(2,1)S(1)} %bitcast.203), channel_id=1, source_target_pairs={{0,16},{16,32},{32,48},{48,64},{64,80},{80,96},{96,112},{1,17},{17... | collective-permute-start | bytes 522248 | tf_op jit(solution)/shard_map/ppermute | solution.py:18
  168.8 3.9 %collective-permute-start.2 = (bf16[66,5,128]{2,1,0:T(8,128)(2,1)S(1)}, bf16[66,5,128]{2,1,0:T(8,128)(2,1)S(1)}, u32[]{:S(2)}, u32[]{:S(2)}) collective-permute-start(bf16[66,5,128]{2,1,0:T(8,128)(2,1)S(1)} %get-tuple-element.164), channel_id=1, source_target_pairs={{0,1},{1,2},{2,3},{3,4},{4,5},{5,6},{6,7},{7,8},{8,9},{9,10},{10,1... | collective-permute-start | bytes 253448 | tf_op jit(solution)/shard_map/ppermute | solution.py:18
  170.8 6.2 %collective-permute-start.3 = (bf16[66,5,128]{2,1,0:T(8,128)(2,1)S(1)}, bf16[66,5,128]{2,1,0:T(8,128)(2,1)S(1)}, u32[]{:S(2)}, u32[]{:S(2)}) collective-permute-start(bf16[66,5,128]{2,1,0:T(8,128)(2,1)S(1)} %get-tuple-element.165), channel_id=1, source_target_pairs={{1,0},{2,1},{3,2},{4,3},{5,4},{6,5},{7,6},{8,7},{9,8},{10,9},{11,1... | collective-permute-start | bytes 253448 | tf_op jit(solution)/shard_map/ppermute | solution.py:20
  (22 other events, 57.7 us)
Sparse Core Ops, SparseCore 0:
  199.6 148.9 all-reduce.1
where the time goes:
time: 358 us; the launch traced here: 357 us
  waiting for transfers between devices  157 us (44%)
  other arithmetic  54.3 us (15%)
  local copies, waits for them, and re-layouts  51.6 us (14%)
  matrix products  48.7 us (14%)
  starting transfers between devices  30.1 us (8%)
  between operations  15.2 us (4%)
    psum x1, waiting for transfers between devices, shards(): lax.psum(jnp.stack(weight_parts).reshape(3, 3, channels, channels), ('lat...  134 us
    mul x8, other arithmetic, accumulate(): lon_matrix[:, :, None] * rows_blk[:, None, :]  41.4 us
    dot_general x8, matrix products, accumulate(): lax.dot_general(lat_matrix, spread, (((0,), (0,)), ((), ())), preferred_e...  28.5 us
    while x48, local copies, waits for them, and re-layouts  17.9 us
    all_to_all x2, starting transfers between devices, one_exchange(): parts = lax.all_to_all(parts, axis, split_axis=0, concat_axis=0, tiled=True)  15.1 us
    all_to_all x2, waiting for transfers between devices, one_exchange(): parts = lax.all_to_all(parts, axis, split_axis=0, concat_axis=0, tiled=True)  13.8 us
    unnamed x33, local copies, waits for them, and re-layouts  12.4 us
    dot_general x9, matrix products, shards(): lax.dot_general(window, flat_grad, (((0,), (0,)), ((), ())), preferred_el...  10.5 us
  transfers between devices with their start and end apart: 11, of which 7 were waited for; matrix products, arithmetic and copies ran while one was open for 30% of the time, Pallas kernels for 0%

commit v1 on v0

--- a/solution.py
+++ b/solution.py
@@ -195,7 +195,7 @@
                 )
             )
     weight_grad = lax.psum(
-        jnp.stack(weight_parts).reshape(3, 3, channels, channels), ("lat", "lon")
+        lax.psum(jnp.stack(weight_parts).reshape(3, 3, channels, channels), "lat"), "lon"
     )
     return (input_grad.reshape(tile_lat, tile_lon, channels).astype(jnp.bfloat16), weight_grad)
 

time: 358 us -> 428 us (1.20)
  waiting for transfers between devices: 157 us -> 221 us
    psum x1 -> x2, waiting for transfers between devices: 134 us -> 198 us  [the longest x1 138 us: shards(): lax.psum(lax.psum(jnp.stack(weight_parts).reshape(3, 3, channels, channel...]
  transfers between devices with their start and end apart: 11 -> 12, of which waited for: 7 -> 8; matrix products, arithmetic and copies ran while one was open for 30% -> 26% of each run, Pallas kernels for 0% -> 0%
where the time goes in v1:
time: 428 us; the launch traced here: 425 us
  waiting for transfers between devices  221 us (52%)
  other arithmetic  54.3 us (13%)
  matrix products  52.7 us (12%)
  local copies, waits for them, and re-layouts  51 us (12%)
  starting transfers between devices  30.4 us (7%)
  between operations  15.2 us (4%)
    psum x1, waiting for transfers between devices, shards(): lax.psum(lax.psum(jnp.stack(weight_parts).reshape(3, 3, channels, channel...  138 us
    psum x1, waiting for transfers between devices, shards(): lax.psum(jnp.stack(weight_parts).reshape(3, 3, channels, channels), 'lat')  60.5 us
    mul x8, other arithmetic, accumulate(): lon_matrix[:, :, None] * rows_blk[:, None, :]  41.4 us
    dot_general x8, matrix products, accumulate(): lax.dot_general(lat_matrix, spread, (((0,), (0,)), ((), ())), preferred_e...  28.5 us
    while x48, local copies, waits for them, and re-layouts  17.9 us
    all_to_all x2, starting transfers between devices, one_exchange(): parts = lax.all_to_all(parts, axis, split_axis=0, concat_axis=0, tiled=True)  15.1 us
    all_to_all x2, waiting for transfers between devices, one_exchange(): parts = lax.all_to_all(parts, axis, split_axis=0, concat_axis=0, tiled=True)  13.8 us
    dot_general x9, matrix products, shards(): lax.dot_general(shifted, conv_weight[a, b], (((1,), (1,)), ((), ())), pre...  13.7 us
  transfers between devices with their start and end apart: 12, of which 8 were waited for; matrix products, arithmetic and copies ran while one was open for 26% of the time, Pallas kernels for 0%

profile of v1, /device:TPU:1, one launch (start us, length us, event | category | flops | bytes accessed | tf_op | source)
XLA Modules:
  0.0 425.0 jit_solution(77586554242475950)
XLA Ops:
  8.0 4.5 %collective-permute-start.5 = (bf16[1,128,128]{2,1,0:T(8,128)(2,1)S(1)}, bf16[1,128,128]{2,1,0:T(8,128)(2,1)S(1)}, u32[]{:S(2)}, u32[]{:S(2)}) collective-permute-start(bf16[1,128,128]{2,1,0:T(8,128)(2,1)S(1)} %get-tuple-element.168), channel_id=1, source_target_pairs={{16,0},{32,16},{48,32},{64,48},{80,64},{96,80},{112,96},{0,112},{1... | collective-permute-start | bytes 98312 | tf_op jit(solution)/shard_map/ppermute | solution.py:20
  22.2 11.0 %all-to-all-start = ((bf16[128,1,1,16,4]{3,4,2,1,0:T(4,128)(2,1)}), bf16[128,1,1,16,4]{3,4,2,1,0:T(4,128)(2,1)S(1)}, u32[]{:S(2)}, u32[]{:S(2)}) async-start(bf16[128,1,1,16,4]{3,4,2,1,0:T(4,128)(2,1)} %copy.87), calls=%async_computation | async-start | bytes 262144 | tf_op jit(solution)/shard_map/all_to_all | solution.py:44
  33.2 4.3 %scatter_custom_fusion.1 = bf16[2048,128]{1,0:T(8,128)(2,1)} fusion(s32[1024]{0:T(1024)S(1)} %bitcast.226, bf16[1024,128]{1,0:T(8,128)(2,1)} %param.18, bf16[]{:T(256)} %constant.168.clone.1), kind=kCustom, calls=%fused_computation.87 | custom fusion | bytes 524800 | tf_op jit(solution)/shard_map/scatter | solution.py:98
  37.5 5.6 %all-to-all-done = bf16[128,1,1,16,4]{3,4,2,1,0:T(4,128)(2,1)S(1)} async-done(((bf16[128,1,1,16,4]{3,4,2,1,0:T(4,128)(2,1)}), bf16[128,1,1,16,4]{3,4,2,1,0:T(4,128)(2,1)S(1)}, u32[]{:S(2)}, u32[]{:S(2)}) %all-to-all-start) | async-done | bytes 16416 | tf_op jit(solution)/shard_map/all_to_all | solution.py:44
  43.1 4.2 all-to-all-start.1
  53.2 8.2 %all-to-all-done.1 = bf16[128,1,1,16,128]{4,3,2,1,0:T(8,128)(2,1)S(1)} async-done(((bf16[128,1,1,16,128]{4,3,2,1,0:T(8,128)(2,1)}), bf16[128,1,1,16,128]{4,3,2,1,0:T(8,128)(2,1)S(1)}, u32[]{:S(2)}, u32[]{:S(2)}) %all-to-all-start.1) | async-done | bytes 524320 | tf_op jit(solution)/shard_map/all_to_all | solution.py:44
  61.4 91.8 %while.17 = (s32[]{:T(128)}, f32[72,17408]{1,0:T(8,128)}, f32[8,256,4]{1,2,0:T(4,128)S(1)}, bf16[8,256,128]{2,1,0:T(8,128)(2,1)S(1)}, s32[]{:T(128)}, /*index=5*/s32[]{:T(128)}) while((s32[]{:T(128)}, f32[72,17408]{1,0:T(8,128)}, f32[8,256,4]{1,2,0:T(4,128)S(1)}, bf16[8,256,128]{2,1,0:T(8,128)(2,1)S(1)}, s32[]{:T(128)}, ...), condition=%wide.region_8.9_spmd.clone, body=%wide.region_5.8_spmd.clone.sunk | while | flops 649949696 | bytes 63582440 | solution.py:151
  61.9 5.2 %broadcast_multiply_fusion.2 = bf16[256,136,128]{2,1,0:T(8,128)(2,1)S(1)} fusion(bf16[256,128]{1,0:T(8,128)(2,1)S(1)} %dynamic-slice_bitcast_fusion.4, bf16[256,136]{1,0:T(8,128)(2,1)S(1)} %copy.129), kind=kLoop, calls=%fused_computation.5.clone.1 | loop fusion | flops 4456448 | bytes 9048064 | tf_op jit(solution)/shard_map/while/body/eval_jaxpr/mul | solution.py:143
  73.4 5.2 %broadcast_multiply_fusion.2 = bf16[256,136,128]{2,1,0:T(8,128)(2,1)S(1)} fusion(bf16[256,128]{1,0:T(8,128)(2,1)S(1)} %dynamic-slice_bitcast_fusion.4, bf16[256,136]{1,0:T(8,128)(2,1)S(1)} %copy.129), kind=kLoop, calls=%fused_computation.5.clone.1 | loop fusion | flops 4456448 | bytes 9048064 | tf_op jit(solution)/shard_map/while/body/eval_jaxpr/mul | solution.py:143
  84.8 5.2 %broadcast_multiply_fusion.2 = bf16[256,136,128]{2,1,0:T(8,128)(2,1)S(1)} fusion(bf16[256,128]{1,0:T(8,128)(2,1)S(1)} %dynamic-slice_bitcast_fusion.4, bf16[256,136]{1,0:T(8,128)(2,1)S(1)} %copy.129), kind=kLoop, calls=%fused_computation.5.clone.1 | loop fusion | flops 4456448 | bytes 9048064 | tf_op jit(solution)/shard_map/while/body/eval_jaxpr/mul | solution.py:143
  90.1 3.6 convolution_add_fusion.10
  96.3 5.2 %broadcast_multiply_fusion.2 = bf16[256,136,128]{2,1,0:T(8,128)(2,1)S(1)} fusion(bf16[256,128]{1,0:T(8,128)(2,1)S(1)} %dynamic-slice_bitcast_fusion.4, bf16[256,136]{1,0:T(8,128)(2,1)S(1)} %copy.129), kind=kLoop, calls=%fused_computation.5.clone.1 | loop fusion | flops 4456448 | bytes 9048064 | tf_op jit(solution)/shard_map/while/body/eval_jaxpr/mul | solution.py:143
  101.5 3.6 convolution_add_fusion.10
  107.8 5.2 %broadcast_multiply_fusion.2 = bf16[256,136,128]{2,1,0:T(8,128)(2,1)S(1)} fusion(bf16[256,128]{1,0:T(8,128)(2,1)S(1)} %dynamic-slice_bitcast_fusion.4, bf16[256,136]{1,0:T(8,128)(2,1)S(1)} %copy.129), kind=kLoop, calls=%fused_computation.5.clone.1 | loop fusion | flops 4456448 | bytes 9048064 | tf_op jit(solution)/shard_map/while/body/eval_jaxpr/mul | solution.py:143
  113.0 3.6 convolution_add_fusion.10
  119.3 5.2 %broadcast_multiply_fusion.2 = bf16[256,136,128]{2,1,0:T(8,128)(2,1)S(1)} fusion(bf16[256,128]{1,0:T(8,128)(2,1)S(1)} %dynamic-slice_bitcast_fusion.4, bf16[256,136]{1,0:T(8,128)(2,1)S(1)} %copy.129), kind=kLoop, calls=%fused_computation.5.clone.1 | loop fusion | flops 4456448 | bytes 9048064 | tf_op jit(solution)/shard_map/while/body/eval_jaxpr/mul | solution.py:143
  124.5 3.6 convolution_add_fusion.10
  130.8 5.2 %broadcast_multiply_fusion.2 = bf16[256,136,128]{2,1,0:T(8,128)(2,1)S(1)} fusion(bf16[256,128]{1,0:T(8,128)(2,1)S(1)} %dynamic-slice_bitcast_fusion.4, bf16[256,136]{1,0:T(8,128)(2,1)S(1)} %copy.129), kind=kLoop, calls=%fused_computation.5.clone.1 | loop fusion | flops 4456448 | bytes 9048064 | tf_op jit(solution)/shard_map/while/body/eval_jaxpr/mul | solution.py:143
  142.2 5.2 %broadcast_multiply_fusion.2 = bf16[256,136,128]{2,1,0:T(8,128)(2,1)S(1)} fusion(bf16[256,128]{1,0:T(8,128)(2,1)S(1)} %dynamic-slice_bitcast_fusion.4, bf16[256,136]{1,0:T(8,128)(2,1)S(1)} %copy.129), kind=kLoop, calls=%fused_computation.5.clone.1 | loop fusion | flops 4456448 | bytes 9048064 | tf_op jit(solution)/shard_map/while/body/eval_jaxpr/mul | solution.py:143
  161.1 4.0 collective-permute-start
  172.8 4.2 collective-permute-done.3
  181.1 7.0 %fusion.129 = (bf16[64,128,128]{2,1,0:T(8,128)(2,1)}, bf16[64,128,128]{2,1,0:T(8,128)(2,1)S(1)}, bf16[64,128,128]{2,1,0:T(8,128)(2,1)}, bf16[64,128,128]{2,1,0:T...) fusion(bf16[66,130,128]{2,1,0:T(8,128)(2,1)S(1)} %get-tuple-ele, ...), kind=kLoop, calls=%fused_computation.153 | loop fusion | bytes 37748736 | tf_op jit(solution)/shard_map/slice | solution.py:182
  212.9 60.5 %all-reduce.3.cloned.1.call-done = f32[3,3,128,128]{3,2,1,0:T(8,128)} async-done(((f32[3,3,128,128]{3,2,1,0:T(8,128)}), f32[3,3,128,128]{3,2,1,0:T(8,128)}) %all-reduce.3.cloned.1.call-update) | async-done | bytes 589840 | tf_op jit(solution)/shard_map/psum | solution.py:198
  278.6 137.7 %all-reduce.5.cloned.1.call-done = f32[3,3,128,128]{3,2,1,0:T(8,128)} async-done(((f32[3,3,128,128]{3,2,1,0:T(8,128)}), f32[3,3,128,128]{3,2,1,0:T(8,128)}) %all-reduce.5.cloned.1.call-update) | async-done | bytes 589840 | tf_op jit(solution)/shard_map/psum | solution.py:197
  (248 shorter events, 102.1 us)
Async XLA Ops:
  7.2 9.6 %copy-start.11 = (s32[1024,1]{0,1:T(1,128)S(1)}, s32[1024,1]{0,1:T(1,128)}, u32[]{:S(2)}) copy-start(s32[1024,1]{0,1:T(1,128)} %param.19) | copy-start | bytes 12292
  8.0 41.9 %collective-permute-start.5 = (bf16[1,128,128]{2,1,0:T(8,128)(2,1)S(1)}, bf16[1,128,128]{2,1,0:T(8,128)(2,1)S(1)}, u32[]{:S(2)}, u32[]{:S(2)}) collective-permute-start(bf16[1,128,128]{2,1,0:T(8,128)(2,1)S(1)} %get-tuple-element.168), channel_id=1, source_target_pairs={{16,0},{32,16},{48,32},{64,48},{80,64},{96,80},{112,96},{0,112},{1... | collective-permute-start | bytes 98312 | tf_op jit(solution)/shard_map/ppermute | solution.py:20
  12.5 35.4 %collective-permute-start.4 = (bf16[1,128,128]{2,1,0:T(8,128)(2,1)S(1)}, bf16[1,128,128]{2,1,0:T(8,128)(2,1)S(1)}, u32[]{:S(2)}, u32[]{:S(2)}) collective-permute-start(bf16[1,128,128]{2,1,0:T(8,128)(2,1)S(1)} %get-tuple-element.169), channel_id=1, source_target_pairs={{0,16},{16,32},{32,48},{48,64},{64,80},{80,96},{96,112},{112,0},{1... | collective-permute-start | bytes 98312 | tf_op jit(solution)/shard_map/ppermute | solution.py:18
  22.2 20.9 %all-to-all-start = ((bf16[128,1,1,16,4]{3,4,2,1,0:T(4,128)(2,1)}), bf16[128,1,1,16,4]{3,4,2,1,0:T(4,128)(2,1)S(1)}, u32[]{:S(2)}, u32[]{:S(2)}) async-start(bf16[128,1,1,16,4]{3,4,2,1,0:T(4,128)(2,1)} %copy.87), calls=%async_computation | async-start | bytes 262144 | tf_op jit(solution)/shard_map/all_to_all | solution.py:44
  43.1 18.3 %all-to-all-start.1 = ((bf16[128,1,1,16,128]{4,3,2,1,0:T(8,128)(2,1)}), bf16[128,1,1,16,128]{4,3,2,1,0:T(8,128)(2,1)S(1)}, u32[]{:S(2)}, u32[]{:S(2)}) async-start(bf16[128,1,1,16,128]{4,3,2,1,0:T(8,128)(2,1)} %bitcast.13), calls=%async_computation.1 | async-start | bytes 1048576 | tf_op jit(solution)/shard_map/all_to_all | solution.py:44
  47.3 226.1 %all-reduce.3.cloned.1.call-start = ((), (), s32[]{:S(2)}) async-start(), calls=%async_computation.2 | async-start | bytes 1179648 | tf_op jit(solution)/shard_map/psum | solution.py:198
  50.0 128.0 %collective-permute-start.6 = (bf16[66,1,128]{2,1,0:T(2,128)(2,1)S(1)}, bf16[66,1,128]{2,1,0:T(2,128)(2,1)S(1)}, u32[]{:S(2)}, u32[]{:S(2)}) collective-permute-start(bf16[66,1,128]{2,1,0:T(2,128)(2,1)S(1)} %get-tuple-element.166), channel_id=1, source_target_pairs={{0,1},{1,2},{2,3},{3,4},{4,5},{5,6},{6,7},{7,8},{8,9},{9,10},{10,1... | collective-permute-start | bytes 50696 | tf_op jit(solution)/shard_map/ppermute | solution.py:18
  53.2 124.8 %collective-permute-start.7 = (bf16[66,1,128]{2,1,0:T(2,128)(2,1)S(1)}, bf16[66,1,128]{2,1,0:T(2,128)(2,1)S(1)}, u32[]{:S(2)}, u32[]{:S(2)}) collective-permute-start(bf16[66,1,128]{2,1,0:T(2,128)(2,1)S(1)} %get-tuple-element.167), channel_id=1, source_target_pairs={{1,0},{2,1},{3,2},{4,3},{5,4},{6,5},{7,6},{8,7},{9,8},{10,9},{11,1... | collective-permute-start | bytes 50696 | tf_op jit(solution)/shard_map/ppermute | solution.py:20
  61.8 5.2 %slice-start = ((s8[5013504]{0:T(1024)(128)(4,1)}), s8[4194304]{0:T(1024)(128)(4,1)S(1)}, s32[]{:S(2)}) async-start(s8[5013504]{0:T(1024)(128)(4,1)} %bitcast.191), calls=%async_computation.4 | async-start | bytes 8388608 | tf_op jit(solution)/shard_map/while
  61.9 5.2 %slice-start.1 = ((s8[5013504]{0:T(1024)(128)(4,1)}), s8[819200]{0:T(1024)(128)(4,1)S(1)}, s32[]{:S(2)}) async-start(s8[5013504]{0:T(1024)(128)(4,1)} %bitcast.191), calls=%async_computation.5 | async-start | bytes 1638400 | tf_op jit(solution)/shard_map/while
  73.3 5.2 %slice-start = ((s8[5013504]{0:T(1024)(128)(4,1)}), s8[4194304]{0:T(1024)(128)(4,1)S(1)}, s32[]{:S(2)}) async-start(s8[5013504]{0:T(1024)(128)(4,1)} %bitcast.191), calls=%async_computation.4 | async-start | bytes 8388608 | tf_op jit(solution)/shard_map/while
  73.4 5.2 %slice-start.1 = ((s8[5013504]{0:T(1024)(128)(4,1)}), s8[819200]{0:T(1024)(128)(4,1)S(1)}, s32[]{:S(2)}) async-start(s8[5013504]{0:T(1024)(128)(4,1)} %bitcast.191), calls=%async_computation.5 | async-start | bytes 1638400 | tf_op jit(solution)/shard_map/while
  84.8 5.2 %slice-start = ((s8[5013504]{0:T(1024)(128)(4,1)}), s8[4194304]{0:T(1024)(128)(4,1)S(1)}, s32[]{:S(2)}) async-start(s8[5013504]{0:T(1024)(128)(4,1)} %bitcast.191), calls=%async_computation.4 | async-start | bytes 8388608 | tf_op jit(solution)/shard_map/while
  96.3 5.2 %slice-start = ((s8[5013504]{0:T(1024)(128)(4,1)}), s8[4194304]{0:T(1024)(128)(4,1)S(1)}, s32[]{:S(2)}) async-start(s8[5013504]{0:T(1024)(128)(4,1)} %bitcast.191), calls=%async_computation.4 | async-start | bytes 8388608 | tf_op jit(solution)/shard_map/while
  107.8 5.2 %slice-start = ((s8[5013504]{0:T(1024)(128)(4,1)}), s8[4194304]{0:T(1024)(128)(4,1)S(1)}, s32[]{:S(2)}) async-start(s8[5013504]{0:T(1024)(128)(4,1)} %bitcast.191), calls=%async_computation.4 | async-start | bytes 8388608 | tf_op jit(solution)/shard_map/while
  119.2 5.2 %slice-start = ((s8[5013504]{0:T(1024)(128)(4,1)}), s8[4194304]{0:T(1024)(128)(4,1)S(1)}, s32[]{:S(2)}) async-start(s8[5013504]{0:T(1024)(128)(4,1)} %bitcast.191), calls=%async_computation.4 | async-start | bytes 8388608 | tf_op jit(solution)/shard_map/while
  119.3 5.2 %slice-start.1 = ((s8[5013504]{0:T(1024)(128)(4,1)}), s8[819200]{0:T(1024)(128)(4,1)S(1)}, s32[]{:S(2)}) async-start(s8[5013504]{0:T(1024)(128)(4,1)} %bitcast.191), calls=%async_computation.5 | async-start | bytes 1638400 | tf_op jit(solution)/shard_map/while
  130.7 5.2 %slice-start = ((s8[5013504]{0:T(1024)(128)(4,1)}), s8[4194304]{0:T(1024)(128)(4,1)S(1)}, s32[]{:S(2)}) async-start(s8[5013504]{0:T(1024)(128)(4,1)} %bitcast.191), calls=%async_computation.4 | async-start | bytes 8388608 | tf_op jit(solution)/shard_map/while
  142.2 5.2 %slice-start = ((s8[5013504]{0:T(1024)(128)(4,1)}), s8[4194304]{0:T(1024)(128)(4,1)S(1)}, s32[]{:S(2)}) async-start(s8[5013504]{0:T(1024)(128)(4,1)} %bitcast.191), calls=%async_computation.4 | async-start | bytes 8388608 | tf_op jit(solution)/shard_map/while
  159.8 7.7 %collective-permute-start.1 = (bf16[5,136,128]{2,1,0:T(8,128)(2,1)S(1)}, bf16[5,136,128]{2,1,0:T(8,128)(2,1)S(1)}, u32[]{:S(2)}, u32[]{:S(2)}) collective-permute-start(bf16[5,136,128]{2,1,0:T(8,128)(2,1)S(1)} %bitcast.207), channel_id=1, source_target_pairs={{16,0},{32,16},{48,32},{64,48},{80,64},{96,80},{112,96},{17,1},{33... | collective-permute-start | bytes 522248 | tf_op jit(solution)/shard_map/ppermute | solution.py:20
  161.1 7.2 %collective-permute-start = (bf16[5,136,128]{2,1,0:T(8,128)(2,1)S(1)}, bf16[5,136,128]{2,1,0:T(8,128)(2,1)S(1)}, u32[]{:S(2)}, u32[]{:S(2)}) collective-permute-start(bf16[5,136,128]{2,1,0:T(8,128)(2,1)S(1)} %bitcast.203), channel_id=1, source_target_pairs={{0,16},{16,32},{32,48},{48,64},{64,80},{80,96},{96,112},{1,17},{17... | collective-permute-start | bytes 522248 | tf_op jit(solution)/shard_map/ppermute | solution.py:18
  168.8 3.9 collective-permute-start.2
  170.8 6.2 %collective-permute-start.3 = (bf16[66,5,128]{2,1,0:T(8,128)(2,1)S(1)}, bf16[66,5,128]{2,1,0:T(8,128)(2,1)S(1)}, u32[]{:S(2)}, u32[]{:S(2)}) collective-permute-start(bf16[66,5,128]{2,1,0:T(8,128)(2,1)S(1)} %get-tuple-element.165), channel_id=1, source_target_pairs={{1,0},{2,1},{3,2},{4,3},{5,4},{6,5},{7,6},{8,7},{9,8},{10,9},{11,1... | collective-permute-start | bytes 253448 | tf_op jit(solution)/shard_map/ppermute | solution.py:20
  199.5 216.7 %all-reduce.5.cloned.1.call-start = ((), (), s32[]{:S(2)}) async-start(), calls=%async_computation.3 | async-start | bytes 1179648 | tf_op jit(solution)/shard_map/psum | solution.py:197
  (23 other events, 64.6 us)
Sparse Core Ops, SparseCore 0:
  199.6 73.7 all-reduce.2
  275.9 140.2 all-reduce.4
